TPU v7x, 256 devices: a whole 4x4x8 slice. The times are simulated.
256 devices in a mesh: depth: 32 (over z, x_hi, core), shot: 8 (over y, x_lo).
Axes of the slice: x: 4 (x_hi: 2, x_lo: 2; x = x_hi * 2 + x_lo), y: 4, z: 8, core: 2. Of those that a mesh axis runs over, the one named last changes fastest.
Arguments:
- courant: float32 [512, 64, 128], P('depth'), may hold values from 0.04 to 0.2
- wave_before: float32 [8, 512, 64, 128], P('shot', 'depth'), may hold values from -10 to 10
- wave_current: float32 [8, 512, 64, 128], P('shot', 'depth'), may hold values from -10 to 10
- adjoint_after: float32 [8, 512, 64, 128], P('shot', 'depth'), may hold values from -10 to 10
- adjoint_current: float32 [8, 512, 64, 128], P('shot', 'depth'), may hold values from -10 to 10
- source_cell: int32 [8], P('shot'), may hold values from 0 to 4194303
- wavelet: float32 [8, 4], P('shot'), may hold values from -15 to 15
- receiver_cell: int32 [8, 256], P('shot'), may hold values from 0 to 4194303
- residual: float32 [8, 4, 256], P('shot'), may hold values from -12 to 12
- history: float32 [2, 5, 512, 64, 128], P(None, None, 'depth', 'shot'), may hold values from -23 to 23, as said below
Outputs:
- gradient: float32 [512, 64, 128], P('depth', 'shot')
- direction: float32 [512, 64, 128], P('depth', 'shot')
- courant_next: float32 [512, 64, 128], P('depth')
Inputs may be any that keep to these rules, and one draw needn't show every extreme that they name: In every pair the sum over all cells of history[0] times history[1] is positive.
All inputs are finite; a program needn't handle non-finite values.
Results may differ from a plain program's by a relative error of at most 0.00026.
Values sent between devices are 32-bit elements; how exact they have to be, the bound alone decides.
A program may use at most 128 MiB of HBM per device.

v0:
```python
import jax
import jax.numpy as jnp
from jax import lax
from jax.sharding import PartitionSpec as P

STEPS = 4
PAIRS = 5
coefficients = (-205.0 / 72.0, 8.0 / 5.0, -1.0 / 5.0, 8.0 / 315.0, -1.0 / 560.0)


def with_halo(cells, sides, width):
    for axis, dim in sides:
        count = lax.axis_size(axis)
        ends = count - 1
        head = lax.slice_in_dim(cells, 0, width, axis=dim)
        tail = lax.slice_in_dim(cells, cells.shape[dim] - width, cells.shape[dim], axis=dim)
        cells = jnp.concatenate(
            [
                lax.ppermute(tail, axis, [(i, (i + 1) % count) for i in range(ends)]),
                cells,
                lax.ppermute(head, axis, [((i + 1) % count, i) for i in range(ends)]),
            ],
            axis=dim,
        )
    return cells


def laplace_core(extended):
    interior = extended[4:-4]
    count_rows = interior.shape[0]
    width_x = interior.shape[1]
    width_y = interior.shape[2]
    padded = jnp.pad(interior, ((0, 0), (4, 4), (4, 4)))
    summed = 3.0 * coefficients[0] * interior
    for reach in range(1, 5):
        weight = coefficients[reach]
        summed = summed + weight * (
            extended[4 + reach : 4 + reach + count_rows]
            + extended[4 - reach : 4 - reach + count_rows]
        )
        summed = summed + weight * (
            padded[:, 4 + reach : 4 + reach + width_x, 4 : 4 + width_y]
            + padded[:, 4 - reach : 4 - reach + width_x, 4 : 4 + width_y]
        )
        summed = summed + weight * (
            padded[:, 4 : 4 + width_x, 4 + reach : 4 + reach + width_y]
            + padded[:, 4 : 4 + width_x, 4 - reach : 4 - reach + width_y]
        )
    return summed


def inject(volume, cell_ids, values, offset):
    count_rows = volume.shape[0]
    plane_size = volume.shape[1] * volume.shape[2]
    depth_row = cell_ids // plane_size - offset
    remainder = cell_ids % plane_size
    inside = (depth_row >= 0) & (depth_row < count_rows)
    row_safe = jnp.clip(depth_row, 0, count_rows - 1)
    return volume.at[row_safe, remainder // volume.shape[2], remainder % volume.shape[2]].add(
        jnp.where(inside, values, jnp.zeros_like(values))
    )


def per_device(
    courant,
    wave_before,
    wave_current,
    adjoint_after,
    adjoint_current,
    source_cell,
    wavelet,
    receiver_cell,
    residual,
    history,
):
    slab_rows = courant.shape[0]
    first_row = lax.axis_index("depth") * slab_rows
    shot_count = lax.axis_size("shot")
    summed = jnp.zeros(courant.shape, jnp.float32)
    laplacians = []
    wave_old = wave_before[0]
    wave_now = wave_current[0]
    for moment in range(STEPS):
        extended = with_halo(wave_now, (("depth", 0),), 4)
        laplacian = laplace_core(extended)
        wave_new = 2.0 * wave_now - wave_old + courant * laplacian
        wave_new = inject(wave_new, source_cell, wavelet[0, moment : moment + 1], first_row)
        laplacians.append(laplacian)
        wave_old, wave_now = (wave_now, wave_new)
    adjoint_old = adjoint_after[0]
    adjoint_now = adjoint_current[0]
    for moment in reversed(range(STEPS)):
        extended = with_halo(courant * adjoint_now, (("depth", 0),), 4)
        adjoint_new = 2.0 * adjoint_now - adjoint_old + laplace_core(extended)
        adjoint_new = inject(adjoint_new, receiver_cell[0], residual[0, moment], first_row)
        summed = summed + adjoint_new * laplacians[moment]
        adjoint_old, adjoint_now = (adjoint_now, adjoint_new)
    grad_piece = lax.psum_scatter(summed, "shot", scatter_dimension=1, tiled=True) * (
        1.0 / (shot_count * STEPS)
    )
    displaced = history[0]
    changes = history[1]
    pair_dots = jnp.sum(displaced * changes, axis=(1, 2, 3))
    last_square = jnp.sum(changes[PAIRS - 1] * changes[PAIRS - 1])
    curvature, last_square = lax.psum((pair_dots, last_square), ("depth", "shot"))
    inverse = 1.0 / curvature
    search = grad_piece
    alphas = [None] * PAIRS
    for number in reversed(range(PAIRS)):
        alphas[number] = inverse[number] * lax.psum(
            jnp.sum(displaced[number] * search), ("depth", "shot")
        )
        search = search - alphas[number] * changes[number]
    scaled = curvature[PAIRS - 1] / last_square * search
    for number in range(PAIRS):
        correction = inverse[number] * lax.psum(
            jnp.sum(changes[number] * scaled), ("depth", "shot")
        )
        scaled = scaled + (alphas[number] - correction) * displaced[number]
    direction = -scaled
    piece_width = grad_piece.shape[1]
    own_courant = lax.dynamic_slice_in_dim(
        courant, lax.axis_index("shot") * piece_width, piece_width, 1
    )
    next_piece = own_courant + 0.05 * direction
    courant_next = lax.all_gather(next_piece, "shot", axis=1, tiled=True)
    return (grad_piece, direction, courant_next)


def solution(mesh):
    return jax.shard_map(
        per_device,
        mesh=mesh,
        in_specs=(
            P("depth", None, None),
            P("shot", "depth", None, None),
            P("shot", "depth", None, None),
            P("shot", "depth", None, None),
            P("shot", "depth", None, None),
            P("shot"),
            P("shot", None),
            P("shot", None),
            P("shot", None, None),
            P(None, None, "depth", "shot", None),
        ),
        out_specs=(P("depth", "shot", None), P("depth", "shot", None), P("depth", None, None)),
        check_vma=False,
    )
```

profile of v0, /device:TPU:32, one launch (start us, length us, event | category | flops | bytes accessed | tf_op | source)
XLA Modules:
  0.0 1052.4 jit_solution(10083528813388528675)
XLA Ops:
  7.2 1.7 slice_bitcast_fusion.1
  8.9 3.9 collective-permute-start.2
  12.9 2.1 collective-permute-start.3
  14.9 1.2 bitcast_multiply_fusion
  16.2 6.2 collective-permute-start
  22.3 1.9 collective-permute-start.1
  24.9 0.6 fusion.387
  28.2 0.8 and_reduce_fusion
  29.0 2.0 collective-permute-done.1
  31.0 1.9 fusion.184
  33.0 23.9 %scatter_fusion = f32[16,64,128]{2,1,0:T(8,128)S(1)} fusion(f32[16,64,128]{2,1,0:T(8,128)S(1)} %fusion.184, s32[256]{0:T(256)S(1)} %bitcast.166, f32[256]{0:T(256)} %get-tuple-element.95), kind=kCustom, calls=%fused_computation | custom fusion | flops 256 | bytes 6144 | tf_op jit(solution)/shard_map/scatter-add | solution.py:59
  57.0 3.7 fusion.344
  60.6 0.7 fusion.380
  61.3 4.0 collective-permute-start.10
  65.4 1.9 collective-permute-start.11
  70.0 0.7 fusion.383
  70.7 6.0 collective-permute-start.4
  76.8 1.9 collective-permute-start.5
  78.7 8.4 fusion.59
  87.1 15.2 %scatter_fusion.1 = f32[16,64,128]{2,1,0:T(8,128)S(1)} fusion(f32[16,64,128]{2,1,0:T(8,128)S(1)} %fusion.59, s32[256]{0:T(256)S(1)} %bitcast.167, f32[256]{0:T(256)S(1)} %get-tuple-element.94), kind=kCustom, calls=%fused_computation.1 | custom fusion | flops 256 | bytes 6144 | tf_op jit(solution)/shard_map/scatter-add | solution.py:59
  102.4 3.8 multiply_add_fusion.1
  106.2 0.7 dynamic-slice.25
  108.8 0.7 fusion.379
  109.5 6.0 collective-permute-start.12
  115.6 1.9 collective-permute-start.13
  117.7 0.8 fusion.382
  118.4 6.0 collective-permute-start.6
  124.5 1.9 collective-permute-start.7
  126.4 2.2 fusion.34
  128.7 15.2 %scatter_fusion.2 = f32[16,64,128]{2,1,0:T(8,128)S(1)} fusion(f32[16,64,128]{2,1,0:T(8,128)S(1)} %fusion.34, s32[256]{0:T(256)S(1)} %bitcast.168, f32[256]{0:T(256)S(1)} %get-tuple-element.93), kind=kCustom, calls=%fused_computation.2 | custom fusion | flops 256 | bytes 6144 | tf_op jit(solution)/shard_map/scatter-add | solution.py:59
  143.9 9.8 multiply_add_fusion
  153.7 0.7 dynamic-slice.26
  156.3 0.7 fusion.378
  157.0 6.0 collective-permute-start.14
  163.1 2.1 collective-permute-start.15
  165.4 0.8 fusion.381
  166.2 6.0 collective-permute-start.8
  172.2 1.9 collective-permute-start.9
  174.2 2.2 fusion.9
  176.4 15.2 %scatter_fusion.3 = f32[16,64,128]{2,1,0:T(8,128)S(1)} fusion(f32[16,64,128]{2,1,0:T(8,128)S(1)} %fusion.9, s32[256]{0:T(256)S(1)} %bitcast.169, f32[256]{0:T(256)S(1)} %get-tuple-element.57), kind=kCustom, calls=%fused_computation.3 | custom fusion | flops 256 | bytes 6144 | tf_op jit(solution)/shard_map/scatter-add | solution.py:59
  191.7 10.4 fusion.87
  202.3 51.7 %reduce-scatter.2.cloned.1.call-done = f32[16,8,128]{2,1,0:T(8,128)} async-done(((f32[16,64,128]{2,1,0:T(8,128)}), f32[16,8,128]{2,1,0:T(8,128)}) %reduce-scatter.2.cloned.1.call-update) | async-done | bytes 65552 | tf_op jit(solution)/shard_map/reduce_scatter | solution.py:98
  254.0 1.5 fusion.362
  255.5 73.4 %all-reduce.9 = (f32[5]{0:T(128)S(1)}, f32[]{:T(128)}) all-reduce(f32[5]{0:T(128)S(1)} %multiply_reduce_fusion, f32[]{:T(128)} %get-tuple-element.55), channel_id=1, replica_groups=mesh['depth'=32,'shot'=8] {'depth','shot'}, use_global_device_ids=true, to_apply=%region_7.8 | all-reduce | flops 6 | bytes 48 | tf_op jit(solution)/shard_map/psum | solution.py:105
  328.8 0.7 fusion.386
  330.8 0.6 fusion.360
  332.0 74.0 %psum.87 = f32[]{:T(128)} all-reduce(f32[]{:T(128)} %fusion.360), channel_id=1, replica_groups=mesh['depth'=32,'shot'=8] {'depth','shot'}, use_global_device_ids=true, to_apply=%region_13.14 | all-reduce | flops 1 | bytes 8 | tf_op jit(solution)/shard_map/psum | solution.py:110
  407.3 0.6 fusion.356
  407.9 74.3 %psum.88 = f32[]{:T(128)} all-reduce(f32[]{:T(128)} %get-tuple-element.53), channel_id=1, replica_groups=mesh['depth'=32,'shot'=8] {'depth','shot'}, use_global_device_ids=true, to_apply=%region_15.16 | all-reduce | flops 1 | bytes 8 | tf_op jit(solution)/shard_map/psum | solution.py:110
  483.4 0.6 fusion.365
  484.0 73.3 %psum.89 = f32[]{:T(128)} all-reduce(f32[]{:T(128)} %get-tuple-element.40), channel_id=1, replica_groups=mesh['depth'=32,'shot'=8] {'depth','shot'}, use_global_device_ids=true, to_apply=%region_17.18 | all-reduce | flops 1 | bytes 8 | tf_op jit(solution)/shard_map/psum | solution.py:110
  559.2 74.3 %all-reduce.8 = (f32[]{:T(128)}, f32[]{:T(128)}) all-reduce(f32[]{:T(128)} %get-tuple-element.51, f32[]{:T(128)} %get-tuple-element.39), channel_id=1, replica_groups=mesh['depth'=32,'shot'=8] {'depth','shot'}, use_global_device_ids=true, to_apply=%region_19.20 | all-reduce | flops 2 | bytes 16 | tf_op jit(solution)/shard_map/psum | solution.py:110
  636.1 0.6 fusion.347
  636.8 73.4 %psum.91 = f32[]{:T(128)} all-reduce(f32[]{:T(128)} %fusion.347), channel_id=1, replica_groups=mesh['depth'=32,'shot'=8] {'depth','shot'}, use_global_device_ids=true, to_apply=%region_21.22 | all-reduce | flops 1 | bytes 8 | tf_op jit(solution)/shard_map/psum | solution.py:116
  711.5 0.6 fusion.351
  712.1 74.2 %psum.92 = f32[]{:T(128)} all-reduce(f32[]{:T(128)} %get-tuple-element.49), channel_id=1, replica_groups=mesh['depth'=32,'shot'=8] {'depth','shot'}, use_global_device_ids=true, to_apply=%region_23.24 | all-reduce | flops 1 | bytes 8 | tf_op jit(solution)/shard_map/psum | solution.py:116
  787.6 0.6 fusion.355
  788.2 73.4 %psum.93 = f32[]{:T(128)} all-reduce(f32[]{:T(128)} %fusion.355), channel_id=1, replica_groups=mesh['depth'=32,'shot'=8] {'depth','shot'}, use_global_device_ids=true, to_apply=%region_25.26 | all-reduce | flops 1 | bytes 8 | tf_op jit(solution)/shard_map/psum | solution.py:116
  862.8 0.6 fusion.359
  863.4 74.2 %psum.94 = f32[]{:T(128)} all-reduce(f32[]{:T(128)} %get-tuple-element.47), channel_id=1, replica_groups=mesh['depth'=32,'shot'=8] {'depth','shot'}, use_global_device_ids=true, to_apply=%region_27.28 | all-reduce | flops 1 | bytes 8 | tf_op jit(solution)/shard_map/psum | solution.py:116
  939.5 73.5 %psum.95 = f32[]{:T(128)} all-reduce(f32[]{:T(128)} %fusion.367), channel_id=1, replica_groups=mesh['depth'=32,'shot'=8] {'depth','shot'}, use_global_device_ids=true, to_apply=%region_29.30 | all-reduce | flops 1 | bytes 8 | tf_op jit(solution)/shard_map/psum | solution.py:116
  1014.2 0.7 multiply_add_fusion.2
  1014.9 29.8 %all_gather.3 = f32[16,64,128]{2,1,0:T(8,128)S(1)} all-gather(f32[16,8,128]{2,1,0:T(8,128)S(1)} %get-tuple-element.45), channel_id=1, replica_groups=mesh['depth'=32,'shot'=8] {'shot'}, dimensions={1}, use_global_device_ids=true | all-gather | bytes 589824 | tf_op jit(solution)/shard_map/all_gather | solution.py:126
  1044.7 0.8 copy.22
  (65 shorter events, 3.8 us)
Async XLA Ops:
  7.2 7.8 copy-start
  7.2 246.8 %reduce-scatter.2.cloned.1.call-start = ((), (), s32[]{:S(2)}) async-start(), calls=%async_computation.1 | async-start | bytes 589824 | tf_op jit(solution)/shard_map/reduce_scatter | solution.py:98
  8.9 48.0 %collective-permute-start.2 = (f32[4,64,128]{2,1,0:T(8,128)}, f32[4,64,128]{2,1,0:T(8,128)S(1)}, u32[]{:S(2)}, u32[]{:S(2)}) collective-permute-start(f32[4,64,128]{2,1,0:T(8,128)} %get-tuple-element.80), channel_id=1, source_target_pairs={{8,0},{16,8},{24,16},{32,24},{40,32},{48,40},{56,48},{64,56},{72,6... | collective-permute-start | bytes 393224 | tf_op jit(solution)/shard_map/ppermute | solution.py:21
  12.8 11.5 %copy-start.14 = (f32[1,4,256]{2,1,0:T(4,128)S(1)}, f32[1,4,256]{2,1,0:T(4,128)}, u32[]{:S(2)}) copy-start(f32[1,4,256]{2,1,0:T(4,128)} %param.24) | copy-start | bytes 12292
  12.8 11.5 %copy-start.15 = (s32[1,256]{1,0:T(1,128)S(1)}, s32[1,256]{1,0:T(1,128)}, u32[]{:S(2)}) copy-start(s32[1,256]{1,0:T(1,128)} %param.23) | copy-start | bytes 3076
  12.8 12.1 %copy-start.13 = (f32[1,4]{1,0:T(1,128)S(1)}, f32[1,4]{1,0:T(1,128)}, u32[]{:S(2)}) copy-start(f32[1,4]{1,0:T(1,128)} %param.22) | copy-start | bytes 52
  12.9 44.1 %collective-permute-start.3 = (f32[4,64,128]{2,1,0:T(8,128)S(1)}, f32[4,64,128]{2,1,0:T(8,128)S(1)}, u32[]{:S(2)}, u32[]{:S(2)}) collective-permute-start(f32[4,64,128]{2,1,0:T(8,128)S(1)} %get-tuple-element.81), channel_id=1, source_target_pairs={{0,8},{8,16},{16,24},{24,32},{32,40},{40,48},{48,56},{56,64},{64,7... | collective-permute-start | bytes 393224 | tf_op jit(solution)/shard_map/ppermute | solution.py:19
  14.9 16.1 %copy-start.12 = (f32[1,16,64,128]{3,2,1,0:T(8,128)S(1)}, f32[1,16,64,128]{3,2,1,0:T(8,128)}, u32[]{:S(2)}) copy-start(f32[1,16,64,128]{3,2,1,0:T(8,128)} %param.19) | copy-start | bytes 1572868
  16.1 12.1 %copy-start.16 = (s32[3]{0:T(128)S(1)}, s32[3]{0:T(128)}, u32[]{:S(2)}) copy-start(s32[3]{0:T(128)} %constant.251.clone.1) | copy-start | bytes 40
  16.1 14.9 %copy-start.3 = (f32[1,16,64,128]{3,2,1,0:T(8,128)S(1)}, f32[1,16,64,128]{3,2,1,0:T(8,128)}, u32[]{:S(2)}) copy-start(f32[1,16,64,128]{3,2,1,0:T(8,128)} %param.20) | copy-start | bytes 1572868
  16.2 12.8 %collective-permute-start = (f32[4,64,128]{2,1,0:T(8,128)S(1)}, f32[4,64,128]{2,1,0:T(8,128)S(1)}, u32[]{:S(2)}, u32[]{:S(2)}) collective-permute-start(f32[4,64,128]{2,1,0:T(8,128)S(1)} %get-tuple-element.82), channel_id=1, source_target_pairs={{8,0},{16,8},{24,16},{32,24},{40,32},{48,40},{56,48},{64,56},{72,6... | collective-permute-start | bytes 393224 | tf_op jit(solution)/shard_map/ppermute | solution.py:21
  22.3 8.7 collective-permute-start.1
  33.0 24.0 %copy-start.2 = (f32[1,16,64,128]{3,2,1,0:T(8,128)S(1)}, f32[1,16,64,128]{3,2,1,0:T(8,128)}, u32[]{:S(2)}) copy-start(f32[1,16,64,128]{3,2,1,0:T(8,128)} %param.18) | copy-start | bytes 1572868
  60.6 18.1 %copy-start.8 = (f32[16,64,128]{2,1,0:T(8,128)}, f32[16,64,128]{2,1,0:T(8,128)S(1)}, u32[]{:S(2)}) copy-start(f32[16,64,128]{2,1,0:T(8,128)S(1)} %get-tuple-element.73) | copy-start | bytes 1572868
  61.3 17.4 %collective-permute-start.10 = (f32[4,64,128]{2,1,0:T(8,128)}, f32[4,64,128]{2,1,0:T(8,128)S(1)}, u32[]{:S(2)}, u32[]{:S(2)}) collective-permute-start(f32[4,64,128]{2,1,0:T(8,128)} %get-tuple-element.71), channel_id=1, source_target_pairs={{8,0},{16,8},{24,16},{32,24},{40,32},{48,40},{56,48},{64,56},{72,6... | collective-permute-start | bytes 393224 | tf_op jit(solution)/shard_map/ppermute | solution.py:21
  65.4 13.3 %collective-permute-start.11 = (f32[4,64,128]{2,1,0:T(8,128)S(1)}, f32[4,64,128]{2,1,0:T(8,128)S(1)}, u32[]{:S(2)}, u32[]{:S(2)}) collective-permute-start(f32[4,64,128]{2,1,0:T(8,128)S(1)} %get-tuple-element.72), channel_id=1, source_target_pairs={{0,8},{8,16},{16,24},{24,32},{32,40},{40,48},{48,56},{56,64},{64,7... | collective-permute-start | bytes 393224 | tf_op jit(solution)/shard_map/ppermute | solution.py:19
  70.7 31.6 %collective-permute-start.4 = (f32[4,64,128]{2,1,0:T(8,128)}, f32[4,64,128]{2,1,0:T(8,128)}, u32[]{:S(2)}, u32[]{:S(2)}) collective-permute-start(f32[4,64,128]{2,1,0:T(8,128)} %get-tuple-element.78), channel_id=1, source_target_pairs={{8,0},{16,8},{24,16},{32,24},{40,32},{48,40},{56,48},{64,56},{72,6... | collective-permute-start | bytes 393224 | tf_op jit(solution)/shard_map/ppermute | solution.py:21
  76.8 25.6 %collective-permute-start.5 = (f32[4,64,128]{2,1,0:T(8,128)}, f32[4,64,128]{2,1,0:T(8,128)}, u32[]{:S(2)}, u32[]{:S(2)}) collective-permute-start(f32[4,64,128]{2,1,0:T(8,128)} %get-tuple-element.79), channel_id=1, source_target_pairs={{0,8},{8,16},{16,24},{24,32},{32,40},{40,48},{48,56},{56,64},{64,7... | collective-permute-start | bytes 393224 | tf_op jit(solution)/shard_map/ppermute | solution.py:19
  106.2 9.4 copy-start.9
  109.5 16.9 %collective-permute-start.12 = (f32[4,64,128]{2,1,0:T(8,128)}, f32[4,64,128]{2,1,0:T(8,128)S(1)}, u32[]{:S(2)}, u32[]{:S(2)}) collective-permute-start(f32[4,64,128]{2,1,0:T(8,128)} %get-tuple-element.68), channel_id=1, source_target_pairs={{8,0},{16,8},{24,16},{32,24},{40,32},{48,40},{56,48},{64,56},{72,6... | collective-permute-start | bytes 393224 | tf_op jit(solution)/shard_map/ppermute | solution.py:21
  115.6 10.8 %collective-permute-start.13 = (f32[4,64,128]{2,1,0:T(8,128)}, f32[4,64,128]{2,1,0:T(8,128)}, u32[]{:S(2)}, u32[]{:S(2)}) collective-permute-start(f32[4,64,128]{2,1,0:T(8,128)} %get-tuple-element.69), channel_id=1, source_target_pairs={{0,8},{8,16},{16,24},{24,32},{32,40},{40,48},{48,56},{56,64},{64,7... | collective-permute-start | bytes 393224 | tf_op jit(solution)/shard_map/ppermute | solution.py:19
  117.5 8.9 copy-start.10
  117.7 8.7 copy-start.5
  118.4 25.5 %collective-permute-start.6 = (f32[4,64,128]{2,1,0:T(8,128)}, f32[4,64,128]{2,1,0:T(8,128)S(1)}, u32[]{:S(2)}, u32[]{:S(2)}) collective-permute-start(f32[4,64,128]{2,1,0:T(8,128)} %get-tuple-element.76), channel_id=1, source_target_pairs={{8,0},{16,8},{24,16},{32,24},{40,32},{48,40},{56,48},{64,56},{72,6... | collective-permute-start | bytes 393224 | tf_op jit(solution)/shard_map/ppermute | solution.py:21
  124.5 19.4 %collective-permute-start.7 = (f32[4,64,128]{2,1,0:T(8,128)}, f32[4,64,128]{2,1,0:T(8,128)S(1)}, u32[]{:S(2)}, u32[]{:S(2)}) collective-permute-start(f32[4,64,128]{2,1,0:T(8,128)} %get-tuple-element.77), channel_id=1, source_target_pairs={{0,8},{8,16},{16,24},{24,32},{32,40},{40,48},{48,56},{56,64},{64,7... | collective-permute-start | bytes 393224 | tf_op jit(solution)/shard_map/ppermute | solution.py:19
  153.7 9.4 copy-start.6
  157.0 17.1 %collective-permute-start.14 = (f32[4,64,128]{2,1,0:T(8,128)}, f32[4,64,128]{2,1,0:T(8,128)S(1)}, u32[]{:S(2)}, u32[]{:S(2)}) collective-permute-start(f32[4,64,128]{2,1,0:T(8,128)} %get-tuple-element.65), channel_id=1, source_target_pairs={{8,0},{16,8},{24,16},{32,24},{40,32},{48,40},{56,48},{64,56},{72,6... | collective-permute-start | bytes 393224 | tf_op jit(solution)/shard_map/ppermute | solution.py:21
  163.1 11.1 %collective-permute-start.15 = (f32[4,64,128]{2,1,0:T(8,128)}, f32[4,64,128]{2,1,0:T(8,128)}, u32[]{:S(2)}, u32[]{:S(2)}) collective-permute-start(f32[4,64,128]{2,1,0:T(8,128)} %get-tuple-element.66), channel_id=1, source_target_pairs={{0,8},{8,16},{16,24},{24,32},{32,40},{40,48},{48,56},{56,64},{64,7... | collective-permute-start | bytes 393224 | tf_op jit(solution)/shard_map/ppermute | solution.py:19
  165.2 9.0 copy-start.7
  165.4 8.8 copy-start.4
  166.2 25.5 %collective-permute-start.8 = (f32[4,64,128]{2,1,0:T(8,128)}, f32[4,64,128]{2,1,0:T(8,128)S(1)}, u32[]{:S(2)}, u32[]{:S(2)}) collective-permute-start(f32[4,64,128]{2,1,0:T(8,128)} %get-tuple-element.74), channel_id=1, source_target_pairs={{8,0},{16,8},{24,16},{32,24},{40,32},{48,40},{56,48},{64,56},{72,6... | collective-permute-start | bytes 393224 | tf_op jit(solution)/shard_map/ppermute | solution.py:21
  172.2 19.4 %collective-permute-start.9 = (f32[4,64,128]{2,1,0:T(8,128)}, f32[4,64,128]{2,1,0:T(8,128)S(1)}, u32[]{:S(2)}, u32[]{:S(2)}) collective-permute-start(f32[4,64,128]{2,1,0:T(8,128)} %get-tuple-element.75), channel_id=1, source_target_pairs={{0,8},{8,16},{16,24},{24,32},{32,40},{40,48},{48,56},{56,64},{64,7... | collective-permute-start | bytes 393224 | tf_op jit(solution)/shard_map/ppermute | solution.py:19
  191.7 10.5 copy-start.1
  255.5 381.3 %copy-start.11 = (f32[16,8,128]{2,1,0:T(8,128)}, f32[16,8,128]{2,1,0:T(8,128)S(1)}, u32[]{:S(2)}) copy-start(f32[16,8,128]{2,1,0:T(8,128)S(1)} %get-tuple-element.102) | copy-start | bytes 196612
Sparse Core Ops, SparseCore 0:
  202.3 51.6 reduce-scatter.1
where the time goes:
time: 1060 us; the launch traced here: 1050 us
  blocking collectives  768 us (72%)
  other arithmetic  122 us (12%)
  starting transfers between devices  60 us (6%)
  waiting for transfers between devices  53.8 us (5%)
  between operations  37.1 us (4%)
  local copies, waits for them, and re-layouts  11.3 us (1%)
    psum x5, blocking collectives, per_device(): lax.psum(jnp.sum(changes[number] * scaled), ('depth', 'shot'))  369 us
    psum x4, blocking collectives, per_device(): lax.psum(jnp.sum(displaced[number] * search), ('depth', 'shot'))  296 us
    psum x1, blocking collectives, per_device(): lax.psum((pair_dots, last_square), ('depth', 'shot'))  73.4 us
    scatter-add x4, other arithmetic, inject(): volume.at[row_safe, remainder // volume.shape[2], remainder % volume.shap...  69.6 us
    reduce_scatter x1, waiting for transfers between devices, per_device(): lax.psum_scatter(summed, 'shot', scatter_dimension=1, tiled=True)  51.7 us
    ppermute x8, starting transfers between devices, with_halo(): lax.ppermute(head, axis, [((i + 1) % count, i) for i in range(ends)])  44.3 us
    all_gather x1, blocking collectives, per_device(): courant_next = lax.all_gather(next_piece, 'shot', axis=1, tiled=True)  29.8 us
  transfers between devices with their start and end apart: 17, of which 2 were waited for; matrix products, arithmetic and copies ran while one was open for 9% of the time, Pallas kernels for 0%

commit v1 on v0

--- a/solution.py
+++ b/solution.py
@@ -102,7 +102,9 @@
     changes = history[1]
     pair_dots = jnp.sum(displaced * changes, axis=(1, 2, 3))
     last_square = jnp.sum(changes[PAIRS - 1] * changes[PAIRS - 1])
-    curvature, last_square = lax.psum((pair_dots, last_square), ("depth", "shot"))
+    curvature, last_square = jax.lax.psum(
+        jax.lax.psum((pair_dots, last_square), axis_name="shot"), "depth"
+    )
     inverse = 1.0 / curvature
     search = grad_piece
     alphas = [None] * PAIRS

time: 1060 us -> 1180 us (1.11)
  blocking collectives: 768 us -> 946 us
  waiting for transfers between devices: 53.8 us -> 0.06 us
    psum x4 -> x5, blocking collectives: 296 us -> 387 us  [per_device(): lax.psum(jnp.sum(displaced[number] * search), ('depth', 'shot'))]
    psum x1 -> x4, blocking collectives: 73.4 us -> 153 us  [the longest x2 116 us: per_device(): jax.lax.psum(jax.lax.psum((pair_dots, last_square), axis_name='shot'), 'd...]
    reduce_scatter x1, waiting for transfers between devices: 51.7 us -> 0.01 us  [per_device(): lax.psum_scatter(summed, 'shot', scatter_dimension=1, tiled=True)]
  transfers between devices with their start and end apart: 17 -> 17, of which waited for: 2 -> 0; matrix products, arithmetic and copies ran while one was open for 9% -> 8% of each run, Pallas kernels for 0% -> 0%
where the time goes in v1:
time: 1180 us; the launch traced here: 1170 us
  blocking collectives  946 us (80%)
  other arithmetic  120 us (10%)
  starting transfers between devices  61.9 us (5%)
  between operations  37.2 us (3%)
    psum x5, blocking collectives, per_device(): lax.psum(jnp.sum(displaced[number] * search), ('depth', 'shot'))  387 us
    psum x5, blocking collectives, per_device(): lax.psum(jnp.sum(changes[number] * scaled), ('depth', 'shot'))  376 us
    psum x2, blocking collectives, per_device(): jax.lax.psum(jax.lax.psum((pair_dots, last_square), axis_name='shot'), 'd...  116 us
    scatter-add x4, other arithmetic, inject(): volume.at[row_safe, remainder // volume.shape[2], remainder % volume.shap...  69.6 us
    ppermute x8, starting transfers between devices, with_halo(): lax.ppermute(head, axis, [((i + 1) % count, i) for i in range(ends)])  46.4 us
    psum x2, blocking collectives, per_device(): jax.lax.psum((pair_dots, last_square), axis_name='shot')  37.1 us
    all_gather x1, blocking collectives, per_device(): courant_next = lax.all_gather(next_piece, 'shot', axis=1, tiled=True)  29.9 us
  transfers between devices with their start and end apart: 17, of which 0 were waited for; matrix products, arithmetic and copies ran while one was open for 8% of the time, Pallas kernels for 0%

profile of v1, /device:TPU:32, one launch (start us, length us, event | category | flops | bytes accessed | tf_op | source)
XLA Modules:
  0.0 1172.7 jit_solution(16783708896906228173)
XLA Ops:
  7.2 1.3 bitcast_multiply_fusion
  8.6 4.0 collective-permute-start
  12.7 1.9 collective-permute-start.1
  14.7 6.0 collective-permute-start.2
  20.7 1.9 collective-permute-start.3
  23.3 0.6 fusion.387
  26.5 0.8 and_reduce_fusion
  27.3 2.0 fusion.184
  29.3 23.9 %scatter_fusion = f32[16,64,128]{2,1,0:T(8,128)S(1)} fusion(f32[16,64,128]{2,1,0:T(8,128)S(1)} %fusion.184, s32[256]{0:T(256)S(1)} %bitcast.166, f32[256]{0:T(256)} %get-tuple-element.91), kind=kCustom, calls=%fused_computation | custom fusion | flops 256 | bytes 6144 | tf_op jit(solution)/shard_map/scatter-add | solution.py:59
  53.3 3.7 fusion.344
  57.0 0.7 dynamic-slice.24
  59.8 6.1 collective-permute-start.10
  65.9 1.9 collective-permute-start.11
  67.8 0.7 fusion.383
  68.5 6.0 collective-permute-start.4
  74.5 1.9 collective-permute-start.5
  76.5 8.4 fusion.59
  84.8 15.2 %scatter_fusion.1 = f32[16,64,128]{2,1,0:T(8,128)S(1)} fusion(f32[16,64,128]{2,1,0:T(8,128)S(1)} %fusion.59, s32[256]{0:T(256)S(1)} %bitcast.167, f32[256]{0:T(256)S(1)} %get-tuple-element.90), kind=kCustom, calls=%fused_computation.1 | custom fusion | flops 256 | bytes 6144 | tf_op jit(solution)/shard_map/scatter-add | solution.py:59
  100.1 2.7 multiply_add_fusion.1
  102.8 6.1 collective-permute-start.12
  108.9 1.9 collective-permute-start.13
  113.5 0.7 fusion.382
  114.3 6.0 collective-permute-start.6
  120.3 1.9 collective-permute-start.7
  122.3 2.0 fusion.34
  124.2 15.2 %scatter_fusion.2 = f32[16,64,128]{2,1,0:T(8,128)S(1)} fusion(f32[16,64,128]{2,1,0:T(8,128)S(1)} %fusion.34, s32[256]{0:T(256)S(1)} %bitcast.168, f32[256]{0:T(256)S(1)} %get-tuple-element.89), kind=kCustom, calls=%fused_computation.2 | custom fusion | flops 256 | bytes 6144 | tf_op jit(solution)/shard_map/scatter-add | solution.py:59
  139.5 9.0 multiply_add_fusion
  148.5 6.1 collective-permute-start.14
  154.5 2.1 collective-permute-start.15
  159.4 0.7 fusion.381
  160.1 6.0 collective-permute-start.8
  166.2 1.9 collective-permute-start.9
  168.1 2.2 fusion.9
  170.3 15.2 %scatter_fusion.3 = f32[16,64,128]{2,1,0:T(8,128)S(1)} fusion(f32[16,64,128]{2,1,0:T(8,128)S(1)} %fusion.9, s32[256]{0:T(256)S(1)} %bitcast.169, f32[256]{0:T(256)S(1)} %get-tuple-element.53), kind=kCustom, calls=%fused_computation.3 | custom fusion | flops 256 | bytes 6144 | tf_op jit(solution)/shard_map/scatter-add | solution.py:59
  185.6 10.3 fusion.87
  196.1 19.0 %psum.98 = f32[5]{0:T(128)S(1)} all-reduce(f32[5]{0:T(128)S(1)} %multiply_reduce_fusion), channel_id=1, replica_groups=mesh['depth'=32,'shot'=8] {'shot'}, use_global_device_ids=true, to_apply=%region_7.8 | all-reduce | flops 5 | bytes 40 | tf_op jit(solution)/shard_map/psum | solution.py:106
  215.1 57.0 %psum.99 = f32[5]{0:T(128)S(1)} all-reduce(f32[5]{0:T(128)S(1)} %psum.98), channel_id=1, replica_groups=mesh['depth'=32,'shot'=8] {'depth'}, use_global_device_ids=true, to_apply=%region_8.9 | all-reduce | flops 5 | bytes 40 | tf_op jit(solution)/shard_map/psum | solution.py:105
  272.1 0.7 slice.1091
  272.7 0.7 fusion.386
  273.4 1.5 fusion.362
  274.9 92.4 %psum.102 = f32[]{:T(128)} all-reduce(f32[]{:T(128)} %get-tuple-element.51), channel_id=1, replica_groups=mesh['depth'=32,'shot'=8] {'depth','shot'}, use_global_device_ids=true, to_apply=%region_13.14 | all-reduce | flops 1 | bytes 8 | tf_op jit(solution)/shard_map/psum | solution.py:112
  368.4 0.6 fusion.360
  369.1 73.6 %psum.103 = f32[]{:T(128)} all-reduce(f32[]{:T(128)} %fusion.360), channel_id=1, replica_groups=mesh['depth'=32,'shot'=8] {'depth','shot'}, use_global_device_ids=true, to_apply=%region_15.16 | all-reduce | flops 1 | bytes 8 | tf_op jit(solution)/shard_map/psum | solution.py:112
  444.0 0.6 fusion.356
  444.7 75.4 %psum.104 = f32[]{:T(128)} all-reduce(f32[]{:T(128)} %get-tuple-element.49), channel_id=1, replica_groups=mesh['depth'=32,'shot'=8] {'depth','shot'}, use_global_device_ids=true, to_apply=%region_17.18 | all-reduce | flops 1 | bytes 8 | tf_op jit(solution)/shard_map/psum | solution.py:112
  521.3 0.6 fusion.365
  521.9 73.3 %psum.105 = f32[]{:T(128)} all-reduce(f32[]{:T(128)} %get-tuple-element.40), channel_id=1, replica_groups=mesh['depth'=32,'shot'=8] {'depth','shot'}, use_global_device_ids=true, to_apply=%region_19.20 | all-reduce | flops 1 | bytes 8 | tf_op jit(solution)/shard_map/psum | solution.py:112
  596.5 0.6 fusion.348
  597.2 18.1 %psum.100 = f32[]{:T(128)} all-reduce(f32[]{:T(128)} %get-tuple-element.39), channel_id=1, replica_groups=mesh['depth'=32,'shot'=8] {'shot'}, use_global_device_ids=true, to_apply=%region_10.11 | all-reduce | flops 1 | bytes 8 | tf_op jit(solution)/shard_map/psum | solution.py:106
  615.3 72.0 %psum.106 = f32[]{:T(128)} all-reduce(f32[]{:T(128)} %get-tuple-element.47), channel_id=1, replica_groups=mesh['depth'=32,'shot'=8] {'depth','shot'}, use_global_device_ids=true, to_apply=%region_21.22 | all-reduce | flops 1 | bytes 8 | tf_op jit(solution)/shard_map/psum | solution.py:112
  687.3 59.2 %psum.101 = f32[]{:T(128)} all-reduce(f32[]{:T(128)} %psum.100), channel_id=1, replica_groups=mesh['depth'=32,'shot'=8] {'depth'}, use_global_device_ids=true, to_apply=%region_11.12 | all-reduce | flops 1 | bytes 8 | tf_op jit(solution)/shard_map/psum | solution.py:105
  749.2 0.6 fusion.347
  749.8 82.6 %psum.107 = f32[]{:T(128)} all-reduce(f32[]{:T(128)} %fusion.347), channel_id=1, replica_groups=mesh['depth'=32,'shot'=8] {'depth','shot'}, use_global_device_ids=true, to_apply=%region_23.24 | all-reduce | flops 1 | bytes 8 | tf_op jit(solution)/shard_map/psum | solution.py:118
  833.7 0.6 fusion.351
  834.3 72.1 %psum.108 = f32[]{:T(128)} all-reduce(f32[]{:T(128)} %get-tuple-element.45), channel_id=1, replica_groups=mesh['depth'=32,'shot'=8] {'depth','shot'}, use_global_device_ids=true, to_apply=%region_25.26 | all-reduce | flops 1 | bytes 8 | tf_op jit(solution)/shard_map/psum | solution.py:118
  907.6 0.6 fusion.355
  908.3 73.9 %psum.109 = f32[]{:T(128)} all-reduce(f32[]{:T(128)} %fusion.355), channel_id=1, replica_groups=mesh['depth'=32,'shot'=8] {'depth','shot'}, use_global_device_ids=true, to_apply=%region_27.28 | all-reduce | flops 1 | bytes 8 | tf_op jit(solution)/shard_map/psum | solution.py:118
  983.4 0.6 fusion.359
  984.0 73.2 %psum.110 = f32[]{:T(128)} all-reduce(f32[]{:T(128)} %get-tuple-element.43), channel_id=1, replica_groups=mesh['depth'=32,'shot'=8] {'depth','shot'}, use_global_device_ids=true, to_apply=%region_29.30 | all-reduce | flops 1 | bytes 8 | tf_op jit(solution)/shard_map/psum | solution.py:118
  1058.6 0.6 fusion.367
  1059.2 74.1 %psum.111 = f32[]{:T(128)} all-reduce(f32[]{:T(128)} %fusion.367), channel_id=1, replica_groups=mesh['depth'=32,'shot'=8] {'depth','shot'}, use_global_device_ids=true, to_apply=%region_31.32 | all-reduce | flops 1 | bytes 8 | tf_op jit(solution)/shard_map/psum | solution.py:118
  1134.6 0.7 multiply_add_fusion.2
  1135.2 29.9 %all_gather.3 = f32[16,64,128]{2,1,0:T(8,128)S(1)} all-gather(f32[16,8,128]{2,1,0:T(8,128)S(1)} %get-tuple-element.41), channel_id=1, replica_groups=mesh['depth'=32,'shot'=8] {'shot'}, dimensions={1}, use_global_device_ids=true | all-gather | bytes 589824 | tf_op jit(solution)/shard_map/all_gather | solution.py:128
  1165.1 0.8 copy.22
  (69 shorter events, 2.7 us)
Async XLA Ops:
  7.2 266.2 %reduce-scatter.2.cloned.1.call-start = ((), (), s32[]{:S(2)}) async-start(), calls=%async_computation.1 | async-start | bytes 589824 | tf_op jit(solution)/shard_map/reduce_scatter | solution.py:98
  7.2 20.1 %copy-start.12 = (f32[1,16,64,128]{3,2,1,0:T(8,128)S(1)}, f32[1,16,64,128]{3,2,1,0:T(8,128)}, u32[]{:S(2)}) copy-start(f32[1,16,64,128]{3,2,1,0:T(8,128)} %param.19) | copy-start | bytes 1572868
  8.5 6.1 copy-start.2
  8.5 14.1 %copy-start.14 = (f32[1,4,256]{2,1,0:T(4,128)S(1)}, f32[1,4,256]{2,1,0:T(4,128)}, u32[]{:S(2)}) copy-start(f32[1,4,256]{2,1,0:T(4,128)} %param.24) | copy-start | bytes 12292
  8.6 14.1 %copy-start.15 = (s32[1,256]{1,0:T(1,128)S(1)}, s32[1,256]{1,0:T(1,128)}, u32[]{:S(2)}) copy-start(s32[1,256]{1,0:T(1,128)} %param.23) | copy-start | bytes 3076
  8.6 14.7 %copy-start.13 = (f32[1,4]{1,0:T(1,128)S(1)}, f32[1,4]{1,0:T(1,128)}, u32[]{:S(2)}) copy-start(f32[1,4]{1,0:T(1,128)} %param.22) | copy-start | bytes 52
  8.6 18.0 %copy-start.16 = (s32[3]{0:T(128)S(1)}, s32[3]{0:T(128)}, u32[]{:S(2)}) copy-start(s32[3]{0:T(128)} %constant.251.clone.1) | copy-start | bytes 40
  8.6 18.7 %copy-start.3 = (f32[1,16,64,128]{3,2,1,0:T(8,128)S(1)}, f32[1,16,64,128]{3,2,1,0:T(8,128)}, u32[]{:S(2)}) copy-start(f32[1,16,64,128]{3,2,1,0:T(8,128)} %param.20) | copy-start | bytes 1572868
  8.6 18.7 %collective-permute-start = (f32[4,64,128]{2,1,0:T(8,128)S(1)}, f32[4,64,128]{2,1,0:T(8,128)S(1)}, u32[]{:S(2)}, u32[]{:S(2)}) collective-permute-start(f32[4,64,128]{2,1,0:T(8,128)S(1)} %get-tuple-element.78), channel_id=1, source_target_pairs={{8,0},{16,8},{24,16},{32,24},{40,32},{48,40},{56,48},{64,56},{72,6... | collective-permute-start | bytes 393224 | tf_op jit(solution)/shard_map/ppermute | solution.py:21
  12.7 14.6 %collective-permute-start.1 = (f32[4,64,128]{2,1,0:T(8,128)S(1)}, f32[4,64,128]{2,1,0:T(8,128)S(1)}, u32[]{:S(2)}, u32[]{:S(2)}) collective-permute-start(f32[4,64,128]{2,1,0:T(8,128)S(1)} %get-tuple-element.79), channel_id=1, source_target_pairs={{0,8},{8,16},{16,24},{24,32},{32,40},{40,48},{48,56},{56,64},{64,7... | collective-permute-start | bytes 393224 | tf_op jit(solution)/shard_map/ppermute | solution.py:19
  14.7 38.6 %collective-permute-start.2 = (f32[4,64,128]{2,1,0:T(8,128)S(1)}, f32[4,64,128]{2,1,0:T(8,128)S(1)}, u32[]{:S(2)}, u32[]{:S(2)}) collective-permute-start(f32[4,64,128]{2,1,0:T(8,128)S(1)} %get-tuple-element.76), channel_id=1, source_target_pairs={{8,0},{16,8},{24,16},{32,24},{40,32},{48,40},{56,48},{64,56},{72,6... | collective-permute-start | bytes 393224 | tf_op jit(solution)/shard_map/ppermute | solution.py:21
  20.7 32.6 %collective-permute-start.3 = (f32[4,64,128]{2,1,0:T(8,128)S(1)}, f32[4,64,128]{2,1,0:T(8,128)S(1)}, u32[]{:S(2)}, u32[]{:S(2)}) collective-permute-start(f32[4,64,128]{2,1,0:T(8,128)S(1)} %get-tuple-element.77), channel_id=1, source_target_pairs={{0,8},{8,16},{16,24},{24,32},{32,40},{40,48},{48,56},{56,64},{64,7... | collective-permute-start | bytes 393224 | tf_op jit(solution)/shard_map/ppermute | solution.py:19
  29.3 24.0 %copy-start = (f32[16,64,128]{2,1,0:T(8,128)S(1)}, f32[16,64,128]{2,1,0:T(8,128)}, u32[]{:S(2)}) copy-start(f32[16,64,128]{2,1,0:T(8,128)} %param.16) | copy-start | bytes 1572868
  57.0 19.5 %copy-start.8 = (f32[16,64,128]{2,1,0:T(8,128)}, f32[16,64,128]{2,1,0:T(8,128)S(1)}, u32[]{:S(2)}) copy-start(f32[16,64,128]{2,1,0:T(8,128)S(1)} %get-tuple-element.69) | copy-start | bytes 1572868
  59.8 16.6 %collective-permute-start.10 = (f32[4,64,128]{2,1,0:T(8,128)S(1)}, f32[4,64,128]{2,1,0:T(8,128)S(1)}, u32[]{:S(2)}, u32[]{:S(2)}) collective-permute-start(f32[4,64,128]{2,1,0:T(8,128)S(1)} %get-tuple-element.67), channel_id=1, source_target_pairs={{8,0},{16,8},{24,16},{32,24},{40,32},{48,40},{56,48},{64,56},{72,6... | collective-permute-start | bytes 393224 | tf_op jit(solution)/shard_map/ppermute | solution.py:21
  65.9 10.6 collective-permute-start.11
  68.5 31.6 %collective-permute-start.4 = (f32[4,64,128]{2,1,0:T(8,128)}, f32[4,64,128]{2,1,0:T(8,128)S(1)}, u32[]{:S(2)}, u32[]{:S(2)}) collective-permute-start(f32[4,64,128]{2,1,0:T(8,128)} %get-tuple-element.74), channel_id=1, source_target_pairs={{8,0},{16,8},{24,16},{32,24},{40,32},{48,40},{56,48},{64,56},{72,6... | collective-permute-start | bytes 393224 | tf_op jit(solution)/shard_map/ppermute | solution.py:21
  74.5 25.6 %collective-permute-start.5 = (f32[4,64,128]{2,1,0:T(8,128)S(1)}, f32[4,64,128]{2,1,0:T(8,128)S(1)}, u32[]{:S(2)}, u32[]{:S(2)}) collective-permute-start(f32[4,64,128]{2,1,0:T(8,128)S(1)} %get-tuple-element.75), channel_id=1, source_target_pairs={{0,8},{8,16},{16,24},{24,32},{32,40},{40,48},{48,56},{56,64},{64,7... | collective-permute-start | bytes 393224 | tf_op jit(solution)/shard_map/ppermute | solution.py:19
  102.8 9.3 copy-start.9
  102.8 19.4 %collective-permute-start.12 = (f32[4,64,128]{2,1,0:T(8,128)S(1)}, f32[4,64,128]{2,1,0:T(8,128)S(1)}, u32[]{:S(2)}, u32[]{:S(2)}) collective-permute-start(f32[4,64,128]{2,1,0:T(8,128)S(1)} %get-tuple-element.64), channel_id=1, source_target_pairs={{8,0},{16,8},{24,16},{32,24},{40,32},{48,40},{56,48},{64,56},{72,6... | collective-permute-start | bytes 393224 | tf_op jit(solution)/shard_map/ppermute | solution.py:21
  108.9 13.4 %collective-permute-start.13 = (f32[4,64,128]{2,1,0:T(8,128)S(1)}, f32[4,64,128]{2,1,0:T(8,128)S(1)}, u32[]{:S(2)}, u32[]{:S(2)}) collective-permute-start(f32[4,64,128]{2,1,0:T(8,128)S(1)} %get-tuple-element.65), channel_id=1, source_target_pairs={{0,8},{8,16},{16,24},{24,32},{32,40},{40,48},{48,56},{56,64},{64,7... | collective-permute-start | bytes 393224 | tf_op jit(solution)/shard_map/ppermute | solution.py:19
  113.5 25.9 %copy-start.5 = (f32[16,64,128]{2,1,0:T(8,128)}, f32[16,64,128]{2,1,0:T(8,128)S(1)}, u32[]{:S(2)}) copy-start(f32[16,64,128]{2,1,0:T(8,128)S(1)} %scatter-add.45) | copy-start | bytes 1572868
  113.5 8.7 copy-start.10
  114.3 25.2 %collective-permute-start.6 = (f32[4,64,128]{2,1,0:T(8,128)}, f32[4,64,128]{2,1,0:T(8,128)S(1)}, u32[]{:S(2)}, u32[]{:S(2)}) collective-permute-start(f32[4,64,128]{2,1,0:T(8,128)} %get-tuple-element.72), channel_id=1, source_target_pairs={{8,0},{16,8},{24,16},{32,24},{40,32},{48,40},{56,48},{64,56},{72,6... | collective-permute-start | bytes 393224 | tf_op jit(solution)/shard_map/ppermute | solution.py:21
  120.3 19.2 %collective-permute-start.7 = (f32[4,64,128]{2,1,0:T(8,128)}, f32[4,64,128]{2,1,0:T(8,128)}, u32[]{:S(2)}, u32[]{:S(2)}) collective-permute-start(f32[4,64,128]{2,1,0:T(8,128)} %get-tuple-element.73), channel_id=1, source_target_pairs={{0,8},{8,16},{16,24},{24,32},{32,40},{40,48},{48,56},{56,64},{64,7... | collective-permute-start | bytes 393224 | tf_op jit(solution)/shard_map/ppermute | solution.py:19
  148.5 9.5 copy-start.6
  148.5 19.6 %collective-permute-start.14 = (f32[4,64,128]{2,1,0:T(8,128)S(1)}, f32[4,64,128]{2,1,0:T(8,128)S(1)}, u32[]{:S(2)}, u32[]{:S(2)}) collective-permute-start(f32[4,64,128]{2,1,0:T(8,128)S(1)} %get-tuple-element.61), channel_id=1, source_target_pairs={{8,0},{16,8},{24,16},{32,24},{40,32},{48,40},{56,48},{64,56},{72,6... | collective-permute-start | bytes 393224 | tf_op jit(solution)/shard_map/ppermute | solution.py:21
  154.5 13.5 %collective-permute-start.15 = (f32[4,64,128]{2,1,0:T(8,128)S(1)}, f32[4,64,128]{2,1,0:T(8,128)}, u32[]{:S(2)}, u32[]{:S(2)}) collective-permute-start(f32[4,64,128]{2,1,0:T(8,128)S(1)} %get-tuple-element.62), channel_id=1, source_target_pairs={{0,8},{8,16},{16,24},{24,32},{32,40},{40,48},{48,56},{56,64},{64,7... | collective-permute-start | bytes 393224 | tf_op jit(solution)/shard_map/ppermute | solution.py:19
  159.4 26.2 %copy-start.4 = (f32[16,64,128]{2,1,0:T(8,128)}, f32[16,64,128]{2,1,0:T(8,128)S(1)}, u32[]{:S(2)}) copy-start(f32[16,64,128]{2,1,0:T(8,128)S(1)} %scatter-add.46) | copy-start | bytes 1572868
  159.4 8.7 copy-start.7
  160.1 25.5 %collective-permute-start.8 = (f32[4,64,128]{2,1,0:T(8,128)}, f32[4,64,128]{2,1,0:T(8,128)S(1)}, u32[]{:S(2)}, u32[]{:S(2)}) collective-permute-start(f32[4,64,128]{2,1,0:T(8,128)} %get-tuple-element.70), channel_id=1, source_target_pairs={{8,0},{16,8},{24,16},{32,24},{40,32},{48,40},{56,48},{64,56},{72,6... | collective-permute-start | bytes 393224 | tf_op jit(solution)/shard_map/ppermute | solution.py:21
  166.2 19.4 %collective-permute-start.9 = (f32[4,64,128]{2,1,0:T(8,128)}, f32[4,64,128]{2,1,0:T(8,128)S(1)}, u32[]{:S(2)}, u32[]{:S(2)}) collective-permute-start(f32[4,64,128]{2,1,0:T(8,128)} %get-tuple-element.71), channel_id=1, source_target_pairs={{0,8},{8,16},{16,24},{24,32},{32,40},{40,48},{48,56},{56,64},{64,7... | collective-permute-start | bytes 393224 | tf_op jit(solution)/shard_map/ppermute | solution.py:19
  185.6 10.4 copy-start.1
  274.9 474.9 %copy-start.11 = (f32[16,8,128]{2,1,0:T(8,128)}, f32[16,8,128]{2,1,0:T(8,128)S(1)}, u32[]{:S(2)}) copy-start(f32[16,8,128]{2,1,0:T(8,128)S(1)} %get-tuple-element.98) | copy-start | bytes 196612
Sparse Core Ops, SparseCore 0:
  196.1 51.9 reduce-scatter.1
